TPU v7x, 512 devices: a whole 4x8x8 slice. The times are simulated.
512 devices in a mesh: pts: 32 (over z_lo, y, core), ctr: 16 (over z_hi, x).
Axes of the slice: x: 4, y: 8, z: 8 (z_hi: 4, z_lo: 2; z = z_hi * 2 + z_lo), core: 2. Of those that a mesh axis runs over, the one named last changes fastest.
Arguments:
- points: bfloat16 [8192, 256], P('pts', 'ctr'), may hold values from -6 to 6
- centres: bfloat16 [8192, 256], P('ctr', 'pts'), may hold values from -6 to 6
- precisions: float32 [256], replicated, may hold values from 9.765625e-05 to 0.01953125
- targets: bfloat16 [8192, 128], P('pts', 'ctr'), may hold values from -6 to 6
Outputs:
- coefficients: float32 [8192, 128], P('ctr')
- residual: float32 [8192, 128], P('ctr')
All inputs are finite; a program needn't handle non-finite values.
Results may differ from a plain program's by a relative error of at most 0.0033.
Values may be sent and summed in bfloat16 or wider, within the bound.
No kernel may reach another device: no remote copies, remote signals or barrier semaphores. Data moves between devices by JAX's collectives and lax.ppermute only.
A program may use at most 64 MiB of HBM per device.

v0:
```python
import math

import jax
import jax.numpy as jnp
from jax import lax
from jax.sharding import PartitionSpec as P

FEATURES = 256
BLOCK = 512
NEWTON = 2


ridge_weight = 0.05
jitter_term = 0.1
highest = lax.Precision.HIGHEST


def block_product(matrices, vectors):
    grouped = vectors.reshape(matrices.shape[0], matrices.shape[1], vectors.shape[1])
    return jnp.einsum("bij,bjr->bir", matrices, grouped, precision=highest).reshape(vectors.shape)


def batched(left, right):
    return jnp.einsum("bij,bjk->bik", left, right, precision=highest)


def on_device(points, centres, precisions, targets):
    full_points, full_targets = (
        lax.all_gather(points, "ctr", axis=1, tiled=True),
        lax.all_gather(targets, "ctr", axis=1, tiled=True),
    )
    full_centres = lax.all_gather(centres, "pts", axis=1, tiled=True)
    total = points.shape[0] * lax.axis_size("pts")
    count_blocks = centres.shape[0] // BLOCK
    point_float = full_points.astype(jnp.float32)
    point_square = jnp.sum(precisions * point_float * point_float, axis=1)
    scaled_points = (point_float * precisions).astype(jnp.bfloat16)
    centre_float = full_centres.astype(jnp.float32)
    centre_square = jnp.sum(precisions * centre_float * centre_float, axis=1)
    scaled_centres = (centre_float * precisions).astype(jnp.bfloat16)
    cross_term = lax.dot_general(
        scaled_points, full_centres, (((1,), (1,)), ((), ())), preferred_element_type=jnp.float32
    )
    kernel_tile = jnp.exp(-(point_square[:, None] + centre_square[None, :] - 2.0 * cross_term))
    grouped_scaled = scaled_centres.reshape(count_blocks, BLOCK, FEATURES)
    grouped_centres = full_centres.reshape(count_blocks, BLOCK, FEATURES)
    block_cross = jnp.einsum(
        "bif,bjf->bij", grouped_scaled, grouped_centres, preferred_element_type=jnp.float32
    )
    grouped_square = centre_square.reshape(count_blocks, BLOCK)
    similar = jnp.exp(
        -(grouped_square[:, :, None] + grouped_square[:, None, :] - 2.0 * block_cross)
    )
    identity = jnp.eye(BLOCK, dtype=jnp.float32)
    blocks = 0.5 * (similar + jnp.swapaxes(similar, 1, 2)) + jitter_term * identity
    scale = jnp.sqrt(jnp.sum(blocks * blocks, axis=(1, 2)))
    current_y = blocks / scale[:, None, None]
    current_z = jnp.broadcast_to(identity, blocks.shape)
    width = BLOCK // lax.axis_size("pts")
    first = lax.axis_index("pts") * width
    rows_iota = lax.broadcasted_iota(jnp.int32, (BLOCK, width), 0)
    cols_iota = lax.broadcasted_iota(jnp.int32, (BLOCK, width), 1)
    identity_cols = jnp.where(rows_iota == cols_iota + first, 1.0, 0.0).astype(jnp.float32)
    for newton_step in range(NEWTON):
        y_columns = lax.dynamic_slice_in_dim(current_y, first, width, 2)
        factor = 3.0 * identity_cols - batched(current_z, y_columns)
        next_y = 0.5 * batched(current_y, factor)
        next_z = 0.5 * batched(current_z, factor)
        if newton_step + 1 < NEWTON:
            current_y, current_z = (
                lax.all_gather(next_y, "pts", axis=2, tiled=True),
                lax.all_gather(next_z, "pts", axis=2, tiled=True),
            )
        else:
            current_z = lax.all_gather(next_z, "pts", axis=2, tiled=True)
    target_float = full_targets.astype(jnp.float32)
    right_part = lax.dot_general(
        kernel_tile, target_float, (((0,), (0,)), ((), ())), precision=highest
    )
    right = lax.psum(right_part, "pts") / math.sqrt(total)
    gradient = block_product(current_z, right)
    residual = gradient
    direction = residual
    norm_now = lax.psum(jnp.sum(residual * residual, axis=0), "ctr")
    spread = block_product(current_z, direction)
    values = lax.psum(
        jnp.dot(kernel_tile, spread, precision=highest).astype(jnp.bfloat16), "ctr"
    ).astype(jnp.float32)
    back_part = lax.dot_general(kernel_tile, values, (((0,), (0,)), ((), ())), precision=highest)
    back = lax.psum(back_part, "pts")
    normal = back / total + ridge_weight * block_product(blocks, spread)
    image = block_product(current_z, normal)
    curve = lax.psum(jnp.sum(direction * image, axis=0), "ctr")
    step_size = norm_now / curve
    solution = step_size * direction
    residual = residual - step_size * image
    return (block_product(current_z, solution), residual)


def solution(mesh):
    in_specs = (P("pts", "ctr"), P("ctr", "pts"), P(), P("pts", "ctr"))
    out_specs = (P("ctr", None), P("ctr", None))
    return jax.shard_map(
        on_device, mesh=mesh, in_specs=in_specs, out_specs=out_specs, check_vma=False
    )
```

profile of v0, /device:TPU:1, one launch (start us, length us, event | category | flops | bytes accessed | tf_op | source)
XLA Modules:
  0.0 932.1 jit_solution(13510429586584781246)
XLA Ops:
  7.2 38.1 %all_gather.18 = bf16[512,256]{0,1:T(8,128)(2,1)S(1)} all-gather(bf16[512,8]{0,1:T(8,128)(2,1)} %param.5), channel_id=1, replica_groups=mesh['pts'=32,'ctr'=16] {'pts'}, dimensions={1}, use_global_device_ids=true | all-gather | bytes 270336 | tf_op jit(solution)/shard_map/all_gather | solution.py:32
  45.5 0.5 fusion.3
  45.9 0.3 copy.6
  46.3 0.9 multiply_reduce_fusion
  47.9 0.2 broadcast_divide_fusion
  48.1 0.6 convolution_subtract_fusion.1
  48.7 1.6 convolution_multiply_fusion.4
  50.4 1.0 convolution_multiply_fusion.5
  51.4 0.6 copy-done.7
  52.0 41.3 %all_gather.23 = bf16[256,128]{0,1:T(8,128)(2,1)S(1)} all-gather(bf16[256,8]{0,1:T(8,128)(2,1)S(1)} %copy-done.7), channel_id=1, replica_groups=mesh['pts'=32,'ctr'=16] {'ctr'}, dimensions={1}, use_global_device_ids=true | all-gather | bytes 69632 | tf_op jit(solution)/shard_map/all_gather | solution.py:30
  93.3 31.9 %all_gather.22 = bf16[256,256]{0,1:T(8,128)(2,1)S(1)} all-gather(bf16[256,16]{0,1:T(8,128)(2,1)S(1)} %copy-done.5), channel_id=1, replica_groups=mesh['pts'=32,'ctr'=16] {'ctr'}, dimensions={1}, use_global_device_ids=true | all-gather | bytes 139264 | tf_op jit(solution)/shard_map/all_gather | solution.py:29
  125.3 0.4 fusion.6
  125.7 0.8 copy-done.1
  126.5 1.3 fusion.29
  127.9 55.8 %all-gather.7.cloned.1.call-done = f32[512,512]{0,1:T(8,128)} async-done(((f32[512,16]{0,1:T(8,128)}), f32[512,512]{0,1:T(8,128)}) %all-gather.7.cloned.1.call-update) | async-done | bytes 1048592 | tf_op jit(solution)/shard_map/all_gather | solution.py:72
  183.7 2.0 convolution_subtract_fusion
  185.7 1.3 convolution_multiply_fusion.3
  187.0 228.8 %all-reduce.5.cloned.1.call-done = f32[512,128]{1,0:T(8,128)} async-done(((f32[512,128]{1,0:T(8,128)}), f32[512,128]{1,0:T(8,128)}) %all-reduce.5.cloned.1.call-update) | async-done | bytes 262160 | tf_op jit(solution)/shard_map/psum | solution.py:80
  415.8 67.9 %all-gather.11.cloned.1.call-done = f32[512,512]{0,1:T(8,128)} async-done(((f32[512,16]{0,1:T(8,128)}), f32[512,512]{0,1:T(8,128)}) %all-gather.11.cloned.1.call-update) | async-done | bytes 1048592 | tf_op jit(solution)/shard_map/all_gather | solution.py:75
  483.7 3.2 fusion.17
  486.8 1.8 fusion.30
  488.7 0.7 copy-done.4
  489.4 1.2 convolution_convert_fusion
  490.6 0.2 all-reduce.9.cloned.1.call-start
  490.8 149.6 %all-reduce.7.cloned.1.call-done = bf16[256,128]{1,0:T(8,128)(2,1)} async-done(((bf16[256,128]{1,0:T(8,128)(2,1)}), bf16[256,128]{1,0:T(8,128)(2,1)}) %all-reduce.7.cloned.1.call-update) | async-done | bytes 65552 | tf_op jit(solution)/shard_map/psum | solution.py:86
  640.4 2.4 fusion.31
  642.8 237.6 %all-reduce.9.cloned.1.call-done = f32[512,128]{1,0:T(8,128)} async-done(((f32[512,128]{1,0:T(8,128)}), f32[512,128]{1,0:T(8,128)}) %all-reduce.9.cloned.1.call-update) | async-done | bytes 262160 | tf_op jit(solution)/shard_map/psum | solution.py:90
  880.4 2.0 fusion.7
  882.4 1.8 multiply_reduce_fusion.1
  884.3 37.8 %all-reduce = (f32[128]{0:T(128)S(1)}, f32[128]{0:T(128)S(1)}) all-reduce(f32[128]{0:T(128)S(1)} %get-tuple-element.3, f32[128]{0:T(128)S(1)} %get-tuple-element.2), channel_id=1, replica_groups=mesh['pts'=32,'ctr'=16] {'ctr'}, use_global_device_ids=true, to_apply=%region_5.6 | all-reduce | flops 256 | bytes 2048 | tf_op jit(solution)/shard_map/psum | solution.py:84
  922.0 0.7 multiply_subtract_fusion
  922.8 2.5 fusion.15
  (29 shorter events, 0.6 us)
Async XLA Ops:
  7.2 120.7 %all-gather.9.cloned.1.call-start = ((), (), s32[]{:S(2)}) async-start(), calls=%async_computation.4 | async-start | bytes 1081344 | tf_op jit(solution)/shard_map/all_gather | solution.py:71
  7.2 38.1 %copy-start.6 = (f32[256]{0:T(256)S(1)}, f32[256]{0:T(256)}, u32[]{:S(2)}) copy-start(f32[256]{0:T(256)} %param.6) | copy-start | bytes 3076
  50.3 133.4 %all-gather.7.cloned.1.call-start = ((), (), s32[]{:S(2)}) async-start(), calls=%async_computation.3 | async-start | bytes 1081344 | tf_op jit(solution)/shard_map/all_gather | solution.py:72
  51.4 0.7 copy-start.7
  51.4 41.9 %copy-start.5 = (bf16[256,16]{0,1:T(8,128)(2,1)S(1)}, bf16[256,16]{0,1:T(8,128)(2,1)}, u32[]{:S(2)}) copy-start(bf16[256,16]{0,1:T(8,128)(2,1)} %param.4) | copy-start | bytes 24580
  51.4 364.4 %all-reduce.5.cloned.1.call-start = ((), (), s32[]{:S(2)}) async-start(), calls=%async_computation | async-start | bytes 524288 | tf_op jit(solution)/shard_map/psum | solution.py:80
  125.7 0.8 copy-start.1
  127.8 355.8 %all-gather.11.cloned.1.call-start = ((), (), s32[]{:S(2)}) async-start(), calls=%async_computation.5 | async-start | bytes 1081344 | tf_op jit(solution)/shard_map/all_gather | solution.py:75
  183.7 2.0 copy-start.3
  187.0 453.4 %all-reduce.7.cloned.1.call-start = ((), (), s32[]{:S(2)}) async-start(), calls=%async_computation.1 | async-start | bytes 131072 | tf_op jit(solution)/shard_map/psum | solution.py:86
  483.7 3.2 copy-start
  486.8 2.5 copy-start.2
  488.7 0.7 copy-start.4
  490.6 389.8 %all-reduce.9.cloned.1.call-start = ((), (), s32[]{:S(2)}) async-start(), calls=%async_computation.2 | async-start | bytes 524288 | tf_op jit(solution)/shard_map/psum | solution.py:90
Sparse Core Ops, SparseCore 0:
  50.4 64.4 all-gather.8
  117.7 65.9 all-gather.6
  187.2 228.5 all-reduce.4
  418.4 65.2 all-gather.10
  490.7 149.6 all-reduce.6
  643.7 236.6 all-reduce.8
where the time goes:
time: 938 us; the launch traced here: 932 us
  waiting for transfers between devices  740 us (79%)
  blocking collectives  149 us (16%)
  matrix products  23.4 us (2%)
  between operations  15 us (2%)
    psum x1, waiting for transfers between devices, on_device(): back = lax.psum(back_part, 'pts')  238 us
    psum x1, waiting for transfers between devices, on_device(): right = lax.psum(right_part, 'pts') / math.sqrt(total)  229 us
    psum x1, waiting for transfers between devices, on_device(): lax.psum(jnp.dot(kernel_tile, spread, precision=highest).astype(jnp.bfloa...  150 us
    all_gather x1, waiting for transfers between devices, on_device(): current_z = lax.all_gather(next_z, 'pts', axis=2, tiled=True)  67.9 us
    all_gather x1, waiting for transfers between devices, on_device(): lax.all_gather(next_z, 'pts', axis=2, tiled=True)  55.8 us
    all_gather x1, blocking collectives, on_device(): lax.all_gather(targets, 'ctr', axis=1, tiled=True)  41.3 us
    all_gather x1, blocking collectives, on_device(): full_centres = lax.all_gather(centres, 'pts', axis=1, tiled=True)  38.1 us
    psum x1, blocking collectives, on_device(): norm_now = lax.psum(jnp.sum(residual * residual, axis=0), 'ctr')  37.8 us
  transfers between devices with their start and end apart: 6, of which 5 were waited for; matrix products, arithmetic and copies ran while one was open for 1% of the time, Pallas kernels for 0%

commit v1 on v0

v1 whole, which is shorter than its diff:
```python
import math

import jax
import jax.numpy as jnp
from jax import lax
from jax.sharding import PartitionSpec as P

BLOCK = 512
ridge_weight = 0.05
jitter_term = 0.1
f32, bf16 = jnp.float32, jnp.bfloat16
highest = lax.Precision.HIGHEST
high = lax.Precision.HIGH


def dot(left, right, dims, precision=highest):
    return lax.dot_general(
        left, right, (dims, ((), ())), precision=precision, preferred_element_type=f32
    )


def gather(part, axis, count):
    return lax.all_to_all(jnp.broadcast_to(part[None], (count,) + part.shape), axis, 0, 0)


def scatter_sum(parts, axis):
    return jnp.sum(lax.all_to_all(parts, axis, 0, 0).astype(f32), axis=0)


def split(value):
    first = value.astype(bf16)
    rest = value - first.astype(f32)
    second = rest.astype(bf16)
    return first, second, (rest - second.astype(f32)).astype(bf16)


def on_device(points, centres, precisions, targets):
    n_pts, n_ctr = lax.axis_size("pts"), lax.axis_size("ctr")
    rows, cols = points.shape[0], centres.shape[0]
    width = targets.shape[1] * n_ctr
    total = rows * n_pts
    feats = points.shape[1]

    own_centres = centres.T
    centres_t = gather(own_centres, "pts", n_pts).reshape(-1, cols)
    own_points = jnp.concatenate([points.T, targets.T], axis=0)
    both = gather(own_points, "ctr", n_ctr)
    points_t = both[:, :feats].reshape(-1, rows)
    targets_t = both[:, feats:].reshape(-1, rows)

    weight = precisions[:, None]
    centre_float = centres_t.astype(f32)
    centre_square = jnp.sum(weight * centre_float * centre_float, axis=0)
    scaled_centres = (centre_float * weight).astype(bf16)
    point_float = points_t.astype(f32)
    point_square = jnp.sum(weight * point_float * point_float, axis=0)
    scaled_points = (point_float * weight).astype(bf16)

    cross_term = dot(scaled_points, centres_t, ((0,), (0,)), None)
    kernel_tile = jnp.exp(-(point_square[:, None] + centre_square[None, :] - 2.0 * cross_term))

    right_part = dot(kernel_tile, targets_t.astype(f32), ((0,), (1,)))
    right_own = scatter_sum(right_part.reshape(n_pts, cols // n_pts, width), "pts")

    block_cross = dot(scaled_centres, centres_t, ((0,), (0,)), None)
    similar = jnp.exp(-(centre_square[:, None] + centre_square[None, :] - 2.0 * block_cross))
    identity = jnp.eye(BLOCK, dtype=f32)
    blocks = 0.5 * (similar + similar.T) + jitter_term * identity
    scale = jnp.sqrt(jnp.sum(blocks * blocks))
    first = blocks / scale
    second = dot(first, first, ((1,), (0,)))
    inner = 0.0625 * second - 0.5625 * first
    root = (
        2.25 * identity
        - 2.4375 * first
        + 1.6875 * second
        + dot(second, inner, ((1,), (0,)))
    )

    right = gather(right_own, "pts", n_pts).reshape(cols, width) / math.sqrt(total)
    gradient = dot(root, right, ((1,), (0,)))
    spread = dot(root, gradient, ((1,), (0,)))
    damped = ridge_weight * dot(blocks, spread, ((1,), (0,)))
    norm_part = jnp.sum(gradient * gradient, axis=0)
    curve_part = jnp.sum(spread * damped, axis=0)

    value_part = dot(kernel_tile, spread, ((1,), (0,))).astype(bf16)
    value_own = scatter_sum(value_part.reshape(n_ctr, rows // n_ctr, width), "ctr")
    sums = jnp.stack(split(norm_part) + split(curve_part))
    sums = jnp.pad(sums, ((0, rows // n_ctr - sums.shape[0]), (0, 0)))
    value_all = gather(jnp.concatenate([value_own.astype(bf16), sums], axis=0), "ctr", n_ctr)
    values = value_all[:, : rows // n_ctr].reshape(rows, width).astype(f32)
    sums = jnp.sum(value_all[:, rows // n_ctr : rows // n_ctr + 6].astype(f32), axis=0)
    norm_now = sums[0] + sums[1] + sums[2]
    curve_ridge = sums[3] + sums[4] + sums[5]

    back_part = dot(kernel_tile, values, ((0,), (0,)))
    back_own = scatter_sum(back_part.reshape(n_pts, cols // n_pts, width), "pts")
    energy_part = jnp.sum(values * values, axis=0)
    extra = jnp.pad(energy_part[None], ((0, 7), (0, 0)))
    back_all = gather(jnp.concatenate([back_own, extra], axis=0), "pts", n_pts)
    back = back_all[:, : cols // n_pts].reshape(cols, width)
    energy = jnp.sum(back_all[:, cols // n_pts], axis=0)

    step_size = norm_now / (energy / total + curve_ridge)
    image = dot(root, back / total + damped, ((1,), (0,)))
    return step_size * spread, gradient - step_size * image


def solution(mesh):
    in_specs = (P("pts", "ctr"), P("ctr", "pts"), P(), P("pts", "ctr"))
    out_specs = (P("ctr", None), P("ctr", None))
    return jax.shard_map(
        on_device, mesh=mesh, in_specs=in_specs, out_specs=out_specs, check_vma=False
    )
```

time: 938 us -> 163 us (0.17)
  waiting for transfers between devices: 740 us -> 53.7 us
  blocking collectives: 149 us -> 34.9 us
  starting transfers between devices: 0.43 us -> 40 us
  between operations: 15 us -> 1.51 us
    psum x3 -> x0, waiting for transfers between devices: 616 us -> none  [the longest x1 238 us: on_device(): back = lax.psum(back_part, 'pts')]
    all_gather x3 -> x0, waiting for transfers between devices: 124 us -> none  [the longest x1 67.9 us: on_device(): current_z = lax.all_gather(next_z, 'pts', axis=2, tiled=True)]
    all_gather x3 -> x0, blocking collectives: 111 us -> none  [the longest x1 41.3 us: on_device(): lax.all_gather(targets, 'ctr', axis=1, tiled=True)]
    all_to_all x0 -> x6, waiting for transfers between devices: none -> 53.7 us  [the longest x3 27.3 us: scatter_sum(): return jnp.sum(lax.all_to_all(parts, axis, 0, 0).astype(f32), axis=0)]
    all_to_all x0 -> x6, starting transfers between devices: none -> 40 us  [the longest x3 21.4 us: gather(): lax.all_to_all(jnp.broadcast_to(part[None], (count,) + part.shape), axis,...]
    psum x1 -> x0, blocking collectives: 37.8 us -> none  [on_device(): norm_now = lax.psum(jnp.sum(residual * residual, axis=0), 'ctr')]
    all_to_all x0 -> x2, blocking collectives: none -> 34.9 us  [gather(): lax.all_to_all(jnp.broadcast_to(part[None], (count,) + part.shape), axis,...]
    dot_general x15 -> x11, matrix products: 23.4 us -> 21.2 us  [dot(): lax.dot_general(left, right, (dims, ((), ())), precision=precision, prefe...]
  transfers between devices with their start and end apart: 6 -> 6, of which waited for: 5 -> 6; matrix products, arithmetic and copies ran while one was open for 1% -> 10% of each run, Pallas kernels for 0% -> 0%
where the time goes in v1:
time: 163 us; the launch traced here: 162 us
  waiting for transfers between devices  53.7 us (33%)
  starting transfers between devices  40 us (25%)
  blocking collectives  34.9 us (21%)
  matrix products  21.2 us (13%)
  local copies, waits for them, and re-layouts  6.57 us (4%)
  other arithmetic  4.52 us (3%)
    all_to_all x2, blocking collectives, gather(): lax.all_to_all(jnp.broadcast_to(part[None], (count,) + part.shape), axis,...  34.9 us
    all_to_all x3, waiting for transfers between devices, scatter_sum(): return jnp.sum(lax.all_to_all(parts, axis, 0, 0).astype(f32), axis=0)  27.3 us
    all_to_all x3, waiting for transfers between devices, gather(): lax.all_to_all(jnp.broadcast_to(part[None], (count,) + part.shape), axis,...  26.4 us
    all_to_all x3, starting transfers between devices, gather(): lax.all_to_all(jnp.broadcast_to(part[None], (count,) + part.shape), axis,...  21.4 us
    dot_general x11, matrix products, dot(): lax.dot_general(left, right, (dims, ((), ())), precision=precision, prefe...  21.2 us
    all_to_all x3, starting transfers between devices, scatter_sum(): return jnp.sum(lax.all_to_all(parts, axis, 0, 0).astype(f32), axis=0)  18.6 us
  transfers between devices with their start and end apart: 6, of which 6 were waited for; matrix products, arithmetic and copies ran while one was open for 10% of the time, Pallas kernels for 0%

profile of v1, /device:TPU:1, one launch (start us, length us, event | category | flops | bytes accessed | tf_op | source)
XLA Modules:
  0.0 162.4 jit_solution(17995393237944470202)
XLA Ops:
  0.6 0.7 pad_maximum_fusion
  1.4 22.9 %all_to_all.40 = bf16[16,24,256]{2,1,0:T(8,128)(2,1)S(1)} all-to-all(bf16[16,24,256]{2,1,0:T(8,128)(2,1)S(1)} %broadcast_in_dim.12), channel_id=1, replica_groups=mesh['pts'=32,'ctr'=16] {'ctr'}, dimensions={0} | all-to-all | bytes 393216 | tf_op jit(solution)/shard_map/all_to_all | solution.py:23
  24.3 0.7 broadcast_in_dim.13
  25.0 10.9 %all-to-all-start.1 = ((bf16[32,8,512]{2,1,0:T(8,128)(2,1)}), bf16[32,8,512]{2,1,0:T(8,128)(2,1)S(1)}, u32[]{:S(2)}, u32[]{:S(2)}) async-start(bf16[32,8,512]{2,1,0:T(8,128)(2,1)} %broadcast_in_dim.13), calls=%async_computation.1 | async-start | bytes 524288 | tf_op jit(solution)/shard_map/all_to_all | solution.py:23
  36.2 11.2 %all-to-all-done.1 = bf16[32,8,512]{2,1,0:T(8,128)(2,1)S(1)} async-done(((bf16[32,8,512]{2,1,0:T(8,128)(2,1)}), bf16[32,8,512]{2,1,0:T(8,128)(2,1)S(1)}, u32[]{:S(2)}, u32[]{:S(2)}) %all-to-all-start.1) | async-done | bytes 262176 | tf_op jit(solution)/shard_map/all_to_all | solution.py:23
  47.6 1.1 fusion.14
  48.9 1.1 fusion.27
  49.9 5.4 %all-to-all-start.2 = ((f32[32,16,128]{2,1,0:T(8,128)}), f32[32,16,128]{2,1,0:T(8,128)S(1)}, u32[]{:S(2)}, u32[]{:S(2)}) async-start(f32[32,16,128]{2,1,0:T(8,128)} %fusion.27), calls=%async_computation.2 | async-start | bytes 524288 | tf_op jit(solution)/shard_map/all_to_all | solution.py:27
  55.7 1.3 copy.21
  57.1 2.5 %multiply_reduce_fusion = (f32[]{:T(128)}, f32[512,512]{0,1:T(8,128)S(1)}) fusion(f32[512,512]{1,0:T(8,128)S(1)} %fusion, f32[512,512]{0,1:T(8,128)} %copy.21, f32[512]{0:T(512)S(1)} %fusion.12), kind=kLoop, calls=%fused_computation.20 | loop fusion | flops 3145727 | bytes 3147780 | tf_op jit(solution)/shard_map/reduce_sum | solution.py:69
  60.2 7.0 %all-to-all-done.2 = f32[32,16,128]{2,1,0:T(8,128)S(1)} async-done(((f32[32,16,128]{2,1,0:T(8,128)}), f32[32,16,128]{2,1,0:T(8,128)S(1)}, u32[]{:S(2)}, u32[]{:S(2)}) %all-to-all-start.2) | async-done | bytes 262176 | tf_op jit(solution)/shard_map/all_to_all | solution.py:27
  67.2 0.7 broadcast_in_dim.14
  68.0 5.1 %all-to-all-start.3 = ((f32[32,16,128]{2,1,0:T(8,128)}), f32[32,16,128]{2,1,0:T(8,128)S(1)}, u32[]{:S(2)}, u32[]{:S(2)}) async-start(f32[32,16,128]{2,1,0:T(8,128)} %broadcast_in_dim.14), calls=%async_computation.3 | async-start | bytes 524288 | tf_op jit(solution)/shard_map/all_to_all | solution.py:23
  73.1 4.5 %fusion.21 = f32[512,512]{1,0:T(8,128)} fusion(f32[512,512]{0,1:T(8,128)S(1)} %get-tuple-element.3, f32[]{:T(128)S(6)} %sqrt.3), kind=kOutput, calls=%fused_computation.35 | convolution fusion | flops 1610874880 | bytes 2097156 | tf_op jit(solution)/shard_map/dot_general | solution.py:17
  77.6 2.6 %copy.22 = f32[512,512]{0,1:T(8,128)} copy(f32[512,512]{1,0:T(8,128)} %fusion.21) | data formatting | bytes 2097152 | tf_op jit(solution)/shard_map/dot_general | solution.py:17
  80.2 3.8 %convolution_add_fusion = f32[512,512]{0,1:T(8,128)S(1)} fusion(f32[512,512]{1,0:T(8,128)} %fusion.21, f32[512,512]{0,1:T(8,128)} %copy.22, f32[512,512]{0,1:T(8,128)S(1)} %get-tuple-element.3, f32[]{:T(128)S(6)} %sqrt.3), kind=kOutput, calls=%fused_computation.2 | convolution fusion | flops 1613758464 | bytes 4194308 | tf_op jit(solution)/shard_map/dot_general | solution.py:17
  84.0 1.0 all-to-all-done.3
  85.0 1.8 %multiply_reduce_fusion.2 = (f32[128]{0:T(128)S(1)}, f32[512,128]{1,0:T(8,128)S(1)}) fusion(f32[512,512]{0,1:T(8,128)S(1)} %convolution_add_fusion, f32[512,128]{1,0:T(8,128)S(1)} %bitcast.87), kind=kOutput, calls=%fused_computation.43 | convolution fusion | flops 402784128 | bytes 1573376 | tf_op jit(solution)/shard_map/dot_general | solution.py:17
  86.9 1.8 %fusion.37 = f32[512,128]{1,0:T(8,128)S(1)} fusion(f32[512,512]{0,1:T(8,128)S(1)} %convolution_add_fusion, f32[512,128]{1,0:T(8,128)S(1)} %get-tuple-element.13), kind=kOutput, calls=%fused_computation.73 | convolution fusion | flops 402653184 | bytes 1572864 | tf_op jit(solution)/shard_map/dot_general | solution.py:17
  88.7 1.8 %multiply_reduce_fusion.1 = (f32[128]{0:T(128)S(1)}, f32[512,128]{1,0:T(8,128)S(1)}) fusion(f32[512,128]{1,0:T(8,128)S(1)} %fusion.37, f32[512,512]{0,1:T(8,128)S(1)} %get-tuple-element.3), kind=kOutput, calls=%fused_computation.42 | convolution fusion | flops 402849664 | bytes 1573376 | tf_op jit(solution)/shard_map/dot_general | solution.py:17
  90.5 1.3 convolution_convert_fusion
  91.8 3.5 %all-to-all-start.4 = ((bf16[16,16,128]{2,1,0:T(8,128)(2,1)}), bf16[16,16,128]{2,1,0:T(8,128)(2,1)S(1)}, u32[]{:S(2)}, u32[]{:S(2)}) async-start(bf16[16,16,128]{2,1,0:T(8,128)(2,1)} %bitcast.12), calls=%async_computation.4 | async-start | bytes 131072 | tf_op jit(solution)/shard_map/all_to_all | solution.py:27
  95.4 8.8 %all-to-all-done.4 = bf16[16,16,128]{2,1,0:T(8,128)(2,1)S(1)} async-done(((bf16[16,16,128]{2,1,0:T(8,128)(2,1)}), bf16[16,16,128]{2,1,0:T(8,128)(2,1)S(1)}, u32[]{:S(2)}, u32[]{:S(2)}) %all-to-all-start.4) | async-done | bytes 65568 | tf_op jit(solution)/shard_map/all_to_all | solution.py:27
  104.2 12.0 %all_to_all.41 = bf16[16,32,128]{2,1,0:T(8,128)(2,1)S(1)} all-to-all(bf16[16,32,128]{2,1,0:T(8,128)(2,1)S(1)} %broadcast_in_dim.15), channel_id=1, replica_groups=mesh['pts'=32,'ctr'=16] {'ctr'}, dimensions={0} | all-to-all | bytes 262144 | tf_op jit(solution)/shard_map/all_to_all | solution.py:23
  116.2 1.1 fusion.38
  117.3 9.8 %all-to-all-start.6 = ((f32[32,16,128]{2,1,0:T(8,128)}), f32[32,16,128]{2,1,0:T(8,128)S(1)}, u32[]{:S(2)}, u32[]{:S(2)}) async-start(f32[32,16,128]{2,1,0:T(8,128)} %fusion.38), calls=%async_computation.6 | async-start | bytes 524288 | tf_op jit(solution)/shard_map/all_to_all | solution.py:27
  127.1 11.5 %all-to-all-done.6 = f32[32,16,128]{2,1,0:T(8,128)S(1)} async-done(((f32[32,16,128]{2,1,0:T(8,128)}), f32[32,16,128]{2,1,0:T(8,128)S(1)}, u32[]{:S(2)}, u32[]{:S(2)}) %all-to-all-start.6) | async-done | bytes 262176 | tf_op jit(solution)/shard_map/all_to_all | solution.py:27
  138.7 0.8 broadcast_in_dim.17
  139.4 5.4 %all-to-all-start.7 = ((f32[32,24,128]{2,1,0:T(8,128)}), f32[32,24,128]{2,1,0:T(8,128)S(1)}, u32[]{:S(2)}, u32[]{:S(2)}) async-start(f32[32,24,128]{2,1,0:T(8,128)} %broadcast_in_dim.17), calls=%async_computation.7 | async-start | bytes 786432 | tf_op jit(solution)/shard_map/all_to_all | solution.py:23
  144.8 14.2 %all-to-all-done.7 = f32[32,24,128]{2,1,0:T(8,128)S(1)} async-done(((f32[32,24,128]{2,1,0:T(8,128)}), f32[32,24,128]{2,1,0:T(8,128)S(1)}, u32[]{:S(2)}, u32[]{:S(2)}) %all-to-all-start.7) | async-done | bytes 393248 | tf_op jit(solution)/shard_map/all_to_all | solution.py:23
  159.1 0.7 broadcast_multiply_fusion
  159.9 2.5 %fusion.1 = f32[512,128]{1,0:T(8,128)} fusion(f32[512,128]{1,0:T(8,128)S(1)} %get-tuple-element.13, f32[512,512]{0,1:T(8,128)S(1)} %convolution_add_fusion, f32[512,128]{1,0:T(8,128)S(1)} %bitcast_add_fusion, f32[128]{0:T(128)S(1)} %fusion.31), kind=kOutput, calls=%fused_computation.7 | convolution fusion | flops 402784256 | bytes 1835520 | tf_op jit(solution)/shard_map/dot_general | solution.py:17
  (30 shorter events, 1.5 us)
Async XLA Ops:
  1.4 22.9 %copy-start.1 = (bf16[512,8]{0,1:T(8,128)(2,1)S(1)}, bf16[512,8]{0,1:T(8,128)(2,1)}, u32[]{:S(2)}) copy-start(bf16[512,8]{0,1:T(8,128)(2,1)} %param.5) | copy-start | bytes 24580
  25.0 10.9 %copy-start.2 = (f32[256]{0:T(256)S(1)}, f32[256]{0:T(256)}, u32[]{:S(2)}) copy-start(f32[256]{0:T(256)} %param.6) | copy-start | bytes 3076
  25.0 22.4 %all-to-all-start.1 = ((bf16[32,8,512]{2,1,0:T(8,128)(2,1)}), bf16[32,8,512]{2,1,0:T(8,128)(2,1)S(1)}, u32[]{:S(2)}, u32[]{:S(2)}) async-start(bf16[32,8,512]{2,1,0:T(8,128)(2,1)} %broadcast_in_dim.13), calls=%async_computation.1 | async-start | bytes 524288 | tf_op jit(solution)/shard_map/all_to_all | solution.py:23
  49.9 17.3 %all-to-all-start.2 = ((f32[32,16,128]{2,1,0:T(8,128)}), f32[32,16,128]{2,1,0:T(8,128)S(1)}, u32[]{:S(2)}, u32[]{:S(2)}) async-start(f32[32,16,128]{2,1,0:T(8,128)} %fusion.27), calls=%async_computation.2 | async-start | bytes 524288 | tf_op jit(solution)/shard_map/all_to_all | solution.py:27
  68.0 17.0 %all-to-all-start.3 = ((f32[32,16,128]{2,1,0:T(8,128)}), f32[32,16,128]{2,1,0:T(8,128)S(1)}, u32[]{:S(2)}, u32[]{:S(2)}) async-start(f32[32,16,128]{2,1,0:T(8,128)} %broadcast_in_dim.14), calls=%async_computation.3 | async-start | bytes 524288 | tf_op jit(solution)/shard_map/all_to_all | solution.py:23
  88.7 1.8 %copy-start = (f32[256,512]{1,0:T(8,128)S(1)}, f32[256,512]{1,0:T(8,128)}, u32[]{:S(2)}) copy-start(f32[256,512]{1,0:T(8,128)} %get-tuple-element.11) | copy-start | bytes 1572868
  91.8 12.4 %all-to-all-start.4 = ((bf16[16,16,128]{2,1,0:T(8,128)(2,1)}), bf16[16,16,128]{2,1,0:T(8,128)(2,1)S(1)}, u32[]{:S(2)}, u32[]{:S(2)}) async-start(bf16[16,16,128]{2,1,0:T(8,128)(2,1)} %bitcast.12), calls=%async_computation.4 | async-start | bytes 131072 | tf_op jit(solution)/shard_map/all_to_all | solution.py:27
  117.3 21.3 %all-to-all-start.6 = ((f32[32,16,128]{2,1,0:T(8,128)}), f32[32,16,128]{2,1,0:T(8,128)S(1)}, u32[]{:S(2)}, u32[]{:S(2)}) async-start(f32[32,16,128]{2,1,0:T(8,128)} %fusion.38), calls=%async_computation.6 | async-start | bytes 524288 | tf_op jit(solution)/shard_map/all_to_all | solution.py:27
  139.4 19.6 %all-to-all-start.7 = ((f32[32,24,128]{2,1,0:T(8,128)}), f32[32,24,128]{2,1,0:T(8,128)S(1)}, u32[]{:S(2)}, u32[]{:S(2)}) async-start(f32[32,24,128]{2,1,0:T(8,128)} %broadcast_in_dim.17), calls=%async_computation.7 | async-start | bytes 786432 | tf_op jit(solution)/shard_map/all_to_all | solution.py:23

commit v2 on v1

v2 whole, which is shorter than its diff:
```python
import math

import jax
import jax.numpy as jnp
from jax import lax
from jax.sharding import Mesh, PartitionSpec as P

BLOCK = 512
ridge_weight = 0.05
jitter_term = 0.1
f32, bf16 = jnp.float32, jnp.bfloat16
high = lax.Precision.HIGH
SPLIT = (("zl", 2), ("y", 8), ("core", 2), ("zh", 4), ("x", 4))
PTS, CTR, COLS = ("zl", "y", "core"), ("zh", "x"), ("zl", "core")


def dot(left, right, dims, precision=high):
    return lax.dot_general(
        left, right, (dims, ((), ())), precision=precision, preferred_element_type=f32
    )


def exchange(parts, axes):
    return lax.all_to_all(parts, axes, 0, 0)


def gather(part, axes, count):
    return exchange(jnp.broadcast_to(part[None], (count,) + part.shape), axes)


def scatter_sum(parts, axes):
    return jnp.sum(exchange(parts, axes).astype(f32), axis=0)


def split(value):
    first = lax.reduce_precision(value, 8, 7)
    rest = value - first
    second = lax.reduce_precision(rest, 8, 7)
    return [t.astype(bf16) for t in (first, second, rest - second)]


def on_device(points, centres, precisions, targets):
    n_y, n_cols, n_ctr = lax.axis_size("y"), 4, 16
    n_pts = n_y * n_cols
    rows, cols, feats = points.shape[0], centres.shape[0], points.shape[1] * n_ctr
    width = targets.shape[1] * n_ctr
    total = rows * n_pts
    group = width // n_cols

    part_feats = points.shape[1]
    both = gather(jnp.concatenate([points.T, targets.T], axis=0), CTR, n_ctr)
    some_centres = gather(centres.T, "y", n_y).reshape(-1, rows)
    half = some_centres.shape[0]
    own_points = both[:, :part_feats].reshape(feats, rows)
    own_targets = both[:, part_feats:].reshape(n_cols, group, rows)
    fixed = jnp.concatenate([own_points, some_centres], axis=0)
    sent = jnp.concatenate(
        [jnp.broadcast_to(fixed[None], (n_cols,) + fixed.shape), own_targets], axis=1
    )
    got = exchange(sent, COLS)
    points_t = got[:, :feats]
    centres_t = got[:, feats : feats + half].reshape(2, 2, n_y, -1, cols)
    centres_t = jnp.swapaxes(centres_t, 1, 2).reshape(feats, cols)
    targets_t = got[:, feats + half :]

    weight = precisions[:, None]
    centre_float = centres_t.astype(f32)
    centre_square = jnp.sum(weight * centre_float * centre_float, axis=0)
    scaled_centres = (centre_float * weight).astype(bf16)
    point_float = points_t.astype(f32)
    point_square = jnp.sum(weight * point_float * point_float, axis=1)
    scaled_points = (point_float * weight).astype(bf16)

    cross_term = jnp.einsum(
        "tfp,fc->tpc", scaled_points, centres_t, preferred_element_type=f32
    )
    kernel_tile = jnp.exp(-(point_square[:, :, None] + centre_square - 2.0 * cross_term))
    right_part = jnp.einsum(
        "tqp,tpc->qc", targets_t.astype(f32), kernel_tile, precision=high
    )
    kernel_tile = kernel_tile.reshape(n_cols * rows, cols)
    right = scatter_sum(right_part.reshape(n_y, group // n_y, cols), "y") / math.sqrt(total)

    forward = dot(scaled_centres, centres_t, ((0,), (0,)), None)
    swapped = dot(centres_t, scaled_centres, ((0,), (0,)), None)
    squares = centre_square[:, None] + centre_square[None, :]
    identity = jnp.eye(BLOCK, dtype=f32)
    blocks = (
        0.5 * (jnp.exp(-(squares - 2.0 * forward)) + jnp.exp(-(squares - 2.0 * swapped)))
        + jitter_term * identity
    )
    scale = jnp.sqrt(jnp.sum(blocks * blocks))
    first = blocks / scale
    second = dot(first, first, ((1,), (0,)))
    inner = 0.0625 * second - 0.5625 * first
    root = (
        2.25 * identity - 2.4375 * first + 1.6875 * second + dot(second, inner, ((1,), (0,)))
    )

    gradient = dot(right, root, ((1,), (0,)))
    spread = dot(gradient, root, ((1,), (0,)))
    damped = ridge_weight * dot(spread, blocks, ((1,), (0,)))
    spread_all = gather(spread, "y", n_y).reshape(group, cols)
    norm_part = jnp.sum(gradient * gradient, axis=1)
    curve_part = jnp.sum(spread * damped, axis=1)

    value_part = dot(spread_all, kernel_tile, ((1,), (1,))).astype(bf16)
    value_own = scatter_sum(value_part.reshape(n_ctr, group // n_ctr, -1), CTR).astype(bf16)
    sums = jnp.concatenate(split(jnp.concatenate([norm_part, curve_part])))
    n_sums = sums.shape[0]
    sums = jnp.broadcast_to(jnp.pad(sums, (0, 128 - n_sums))[None], (group // n_ctr, 128))
    value_all = gather(jnp.concatenate([value_own, sums], axis=1), CTR, n_ctr)
    values = value_all[:, :, :-128].reshape(group, -1).astype(f32)
    sums = jnp.sum(value_all[:, 0, -128:].astype(f32), axis=0)[:n_sums]
    sums = jnp.sum(sums.reshape(3, 2, -1), axis=0)
    norm_now, curve_ridge = sums[0], sums[1]

    back_part = dot(values, kernel_tile, ((1,), (0,)))
    energy_part = jnp.sum(values * values, axis=1, keepdims=True)
    back_part = jnp.concatenate(
        [back_part, jnp.broadcast_to(energy_part, (group, 128))], axis=1
    )
    back = scatter_sum(back_part.reshape(n_y, group // n_y, -1), "y") / total
    step_size = norm_now[:, None] / (back[:, -128:-127] + curve_ridge[:, None])
    image = dot(back[:, :-128] + damped, root, ((1,), (0,)))
    own = jnp.concatenate([step_size * spread, gradient - step_size * image], axis=0)
    every = gather(own, COLS + ("y",), n_pts).reshape(n_pts, 2, -1, cols)
    every = jnp.transpose(every, (1, 3, 0, 2)).reshape(2, cols, width)
    return every[0], every[1]


def solution(mesh):
    names, sizes = zip(*SPLIT)
    fine = Mesh(mesh.devices.reshape(sizes), names)
    in_specs = (P(PTS, CTR), P(CTR, PTS), P(), P(PTS, CTR))
    out_specs = (P(CTR, None), P(CTR, None))
    return jax.shard_map(
        on_device, mesh=fine, in_specs=in_specs, out_specs=out_specs, check_vma=False
    )
```

time: 163 us -> 156 us (0.957)
  matrix products: 21.2 us -> 12.1 us
  blocking collectives: 34.9 us -> 37.2 us
  other arithmetic: 4.52 us -> 2.77 us
  waiting for transfers between devices: 53.7 us -> 52 us
  local copies, waits for them, and re-layouts: 6.57 us -> 8.27 us
    dot_general x11 -> x10, matrix products: 21.2 us -> 10.9 us  [dot(): lax.dot_general(left, right, (dims, ((), ())), precision=precision, prefe...]
    dot_general x1 -> x0, local copies, waits for them, and re-layouts: 2.59 us -> none  [dot(): lax.dot_general(left, right, (dims, ((), ())), precision=precision, prefe...]
    all_to_all x2, blocking collectives: 34.9 us -> 37.2 us  [exchange(): return lax.all_to_all(parts, axes, 0, 0)]
    reduce_sum x8 -> x7, other arithmetic: 2.8 us -> 0.5 us  [the longest x1 0.25 us: on_device(): point_square = jnp.sum(weight * point_float * point_float, axis=1)]
    reshape x0 -> x9, local copies, waits for them, and re-layouts: none -> 2.27 us  [the longest x1 0.68 us: on_device(): value_part.reshape(n_ctr, group // n_ctr, -1)]
    all_to_all x6 -> x7, waiting for transfers between devices: 53.7 us -> 52 us  [exchange(): return lax.all_to_all(parts, axes, 0, 0)]
    unnamed x6, local copies, waits for them, and re-layouts: 0.01 us -> 1.68 us
    all_to_all x6 -> x7, starting transfers between devices: 40 us -> 41.5 us  [exchange(): return lax.all_to_all(parts, axes, 0, 0)]
  transfers between devices with their start and end apart: 6 -> 7, of which waited for: 6 -> 7; matrix products, arithmetic and copies ran while one was open for 10% -> 4% of each run, Pallas kernels for 0% -> 0%
where the time goes in v2:
time: 156 us; the launch traced here: 155 us
  waiting for transfers between devices  52 us (33%)
  starting transfers between devices  41.5 us (27%)
  blocking collectives  37.2 us (24%)
  matrix products  12.1 us (8%)
  local copies, waits for them, and re-layouts  8.27 us (5%)
  other arithmetic  2.77 us (2%)
  between operations  1.62 us (1%)
    all_to_all x7, waiting for transfers between devices, exchange(): return lax.all_to_all(parts, axes, 0, 0)  52 us
    all_to_all x7, starting transfers between devices, exchange(): return lax.all_to_all(parts, axes, 0, 0)  41.5 us
    all_to_all x2, blocking collectives, exchange(): return lax.all_to_all(parts, axes, 0, 0)  37.2 us
    dot_general x10, matrix products, dot(): lax.dot_general(left, right, (dims, ((), ())), precision=precision, prefe...  10.9 us
  transfers between devices with their start and end apart: 7, of which 7 were waited for; matrix products, arithmetic and copies ran while one was open for 4% of the time, Pallas kernels for 0%

profile of v2, /device:TPU:1, one launch (start us, length us, event | category | flops | bytes accessed | tf_op | source)
XLA Modules:
  0.0 155.4 jit_solution(5403781251158210967)
XLA Ops:
  0.6 1.3 broadcast_in_dim.19
  2.0 7.6 %all-to-all-start.1 = ((bf16[8,8,512]{2,1,0:T(8,128)(2,1)}), bf16[8,8,512]{2,1,0:T(8,128)(2,1)S(1)}, u32[]{:S(2)}, u32[]{:S(2)}) async-start(bf16[8,8,512]{2,1,0:T(8,128)(2,1)} %broadcast_in_dim.19), calls=%async_computation.1 | async-start | bytes 131072 | tf_op jit(solution)/shard_map/all_to_all | solution.py:24
  9.6 0.7 pad_maximum_fusion.4
  10.3 6.5 %all-to-all-done.1 = bf16[8,8,512]{2,1,0:T(8,128)(2,1)S(1)} async-done(((bf16[8,8,512]{2,1,0:T(8,128)(2,1)}), bf16[8,8,512]{2,1,0:T(8,128)(2,1)S(1)}, u32[]{:S(2)}, u32[]{:S(2)}) %all-to-all-start.1) | async-done | bytes 65568 | tf_op jit(solution)/shard_map/all_to_all | solution.py:24
  16.8 0.7 broadcast_in_dim.18
  17.5 12.6 %all-to-all-start = ((bf16[16,24,256]{2,1,0:T(8,128)(2,1)}), bf16[16,24,256]{2,1,0:T(8,128)(2,1)S(1)}, u32[]{:S(2)}, u32[]{:S(2)}) async-start(bf16[16,24,256]{2,1,0:T(8,128)(2,1)} %broadcast_in_dim.18), calls=%async_computation | async-start | bytes 393216 | tf_op jit(solution)/shard_map/all_to_all | solution.py:24
  30.2 9.7 %all-to-all-done = bf16[16,24,256]{2,1,0:T(8,128)(2,1)S(1)} async-done(((bf16[16,24,256]{2,1,0:T(8,128)(2,1)}), bf16[16,24,256]{2,1,0:T(8,128)(2,1)S(1)}, u32[]{:S(2)}, u32[]{:S(2)}) %all-to-all-start) | async-done | bytes 196640 | tf_op jit(solution)/shard_map/all_to_all | solution.py:24
  39.9 1.0 pad_maximum_fusion
  40.9 7.7 %all-to-all-start.2 = ((bf16[4,416,256]{2,1,0:T(8,128)(2,1)}), bf16[4,416,256]{2,1,0:T(8,128)(2,1)S(1)}, u32[]{:S(2)}, u32[]{:S(2)}) async-start(bf16[4,416,256]{2,1,0:T(8,128)(2,1)} %pad_maximum_fusion), calls=%async_computation.2 | async-start | bytes 1703936 | tf_op jit(solution)/shard_map/all_to_all | solution.py:24
  48.7 11.3 %all-to-all-done.2 = bf16[4,416,256]{2,1,0:T(8,128)(2,1)S(1)} async-done(((bf16[4,416,256]{2,1,0:T(8,128)(2,1)}), bf16[4,416,256]{2,1,0:T(8,128)(2,1)S(1)}, u32[]{:S(2)}, u32[]{:S(2)}) %all-to-all-start.2) | async-done | bytes 852000 | tf_op jit(solution)/shard_map/all_to_all | solution.py:24
  60.7 2.2 %multiply_reduce_fusion = (f32[]{:T(128)}, f32[512,512]{1,0:T(8,128)}) fusion(f32[512,512]{1,0:T(8,128)S(1)} %fusion.8, bf16[2,2,8,8,512]{4,3,2,1,0:T(8,128)(2,1)S(1)} %reshape.91, f32[2,8,2,8]{3,2,1,0:T(2,128)S(1)} %mul.128, f32[512]{0:T(512)S(1)} %fusion.14), kind=kOutput, calls=%fused_computation.26 | convolution fusion | flops 137494528 | bytes 2362372 | tf_op jit(solution)/shard_map/dot_general | solution.py:18
  63.8 0.7 negate_exponential_fusion
  65.1 0.7 reshape.93
  65.7 3.4 %all-to-all-start.3 = ((f32[8,4,512]{2,1,0:T(4,128)}), f32[8,4,512]{2,1,0:T(4,128)S(1)}, u32[]{:S(2)}, u32[]{:S(2)}) async-start(f32[8,4,512]{2,1,0:T(4,128)} %reshape.93), calls=%async_computation.3 | async-start | bytes 131072 | tf_op jit(solution)/shard_map/all_to_all | solution.py:24
  69.1 2.7 %fusion.19 = f32[512,512]{1,0:T(8,128)S(1)} fusion(f32[512,512]{1,0:T(8,128)} %get-tuple-element.23, f32[]{:T(128)S(6)} %sqrt.3), kind=kOutput, calls=%fused_computation.37 | convolution fusion | flops 805568512 | bytes 2097156 | tf_op jit(solution)/shard_map/dot_general | solution.py:18
  71.7 1.2 convolution_add_fusion
  72.9 3.3 %all-to-all-done.3 = f32[8,4,512]{2,1,0:T(4,128)S(1)} async-done(((f32[8,4,512]{2,1,0:T(4,128)}), f32[8,4,512]{2,1,0:T(4,128)S(1)}, u32[]{:S(2)}, u32[]{:S(2)}) %all-to-all-start.3) | async-done | bytes 65568 | tf_op jit(solution)/shard_map/all_to_all | solution.py:24
  77.1 0.6 broadcast_in_dim.21
  77.7 3.4 %all-to-all-start.4 = ((f32[8,4,512]{2,1,0:T(4,128)}), f32[8,4,512]{2,1,0:T(4,128)S(1)}, u32[]{:S(2)}, u32[]{:S(2)}) async-start(f32[8,4,512]{2,1,0:T(4,128)} %broadcast_in_dim.21), calls=%async_computation.4 | async-start | bytes 131072 | tf_op jit(solution)/shard_map/all_to_all | solution.py:24
  81.1 1.7 %multiply_reduce_fusion.2 = (f32[4]{0:T(128)S(1)}, f32[4,512]{1,0:T(4,128)S(1)}) fusion(f32[4,512]{1,0:T(4,128)S(1)} %fusion.37, f32[512,512]{1,0:T(8,128)} %get-tuple-element.23), kind=kOutput, calls=%fused_computation.50 | convolution fusion | flops 6297596 | bytes 1064976 | tf_op jit(solution)/shard_map/dot_general | solution.py:18
  82.8 5.4 %all-to-all-done.4 = f32[8,4,512]{2,1,0:T(4,128)S(1)} async-done(((f32[8,4,512]{2,1,0:T(4,128)}), f32[8,4,512]{2,1,0:T(4,128)S(1)}, u32[]{:S(2)}, u32[]{:S(2)}) %all-to-all-start.4) | async-done | bytes 65568 | tf_op jit(solution)/shard_map/all_to_all | solution.py:24
  88.3 1.0 convolution_convert_fusion
  89.3 0.7 reshape.96
  89.9 3.5 %all-to-all-start.5 = ((bf16[16,2,1024]{2,1,0:T(2,128)(2,1)}), bf16[16,2,1024]{2,1,0:T(2,128)(2,1)S(1)}, u32[]{:S(2)}, u32[]{:S(2)}) async-start(bf16[16,2,1024]{2,1,0:T(2,128)(2,1)} %reshape.96), calls=%async_computation.5 | async-start | bytes 131072 | tf_op jit(solution)/shard_map/all_to_all | solution.py:24
  93.6 8.8 %all-to-all-done.5 = bf16[16,2,1024]{2,1,0:T(2,128)(2,1)S(1)} async-done(((bf16[16,2,1024]{2,1,0:T(2,128)(2,1)}), bf16[16,2,1024]{2,1,0:T(2,128)(2,1)S(1)}, u32[]{:S(2)}, u32[]{:S(2)}) %all-to-all-start.5) | async-done | bytes 65568 | tf_op jit(solution)/shard_map/all_to_all | solution.py:24
  102.5 11.6 %all_to_all.45 = bf16[16,2,1152]{2,1,0:T(2,128)(2,1)S(1)} all-to-all(bf16[16,2,1152]{2,1,0:T(2,128)(2,1)S(1)} %broadcast_in_dim.23), channel_id=1, replica_groups=mesh['zl'=2,'y'=8,'core'=2,'zh'=4,'x'=4] {'zh','x'}, dimensions={0} | all-to-all | bytes 147456 | tf_op jit(solution)/shard_map/all_to_all | solution.py:24
  115.1 0.7 reshape.99
  115.8 3.4 %all-to-all-start.7 = ((f32[8,4,640]{2,1,0:T(4,128)}), f32[8,4,640]{2,1,0:T(4,128)S(1)}, u32[]{:S(2)}, u32[]{:S(2)}) async-start(f32[8,4,640]{2,1,0:T(4,128)} %reshape.99), calls=%async_computation.7 | async-start | bytes 163840 | tf_op jit(solution)/shard_map/all_to_all | solution.py:24
  119.4 7.1 %all-to-all-done.7 = f32[8,4,640]{2,1,0:T(4,128)S(1)} async-done(((f32[8,4,640]{2,1,0:T(4,128)}), f32[8,4,640]{2,1,0:T(4,128)S(1)}, u32[]{:S(2)}, u32[]{:S(2)}) %all-to-all-start.7) | async-done | bytes 81952 | tf_op jit(solution)/shard_map/all_to_all | solution.py:24
  127.2 25.7 %all_to_all.46 = f32[32,8,512]{2,1,0:T(8,128)S(1)} all-to-all(f32[32,8,512]{2,1,0:T(8,128)S(1)} %broadcast_in_dim.26), channel_id=1, replica_groups=mesh['zl'=2,'y'=8,'core'=2,'zh'=4,'x'=4] {'zl','core','y'}, dimensions={0} | all-to-all | bytes 1048576 | tf_op jit(solution)/shard_map/all_to_all | solution.py:24
  153.5 0.8 copy.72
  154.6 0.8 copy.71
  (56 shorter events, 5.7 us)
Async XLA Ops:
  2.0 14.9 %all-to-all-start.1 = ((bf16[8,8,512]{2,1,0:T(8,128)(2,1)}), bf16[8,8,512]{2,1,0:T(8,128)(2,1)S(1)}, u32[]{:S(2)}, u32[]{:S(2)}) async-start(bf16[8,8,512]{2,1,0:T(8,128)(2,1)} %broadcast_in_dim.19), calls=%async_computation.1 | async-start | bytes 131072 | tf_op jit(solution)/shard_map/all_to_all | solution.py:24
  17.5 22.3 %all-to-all-start = ((bf16[16,24,256]{2,1,0:T(8,128)(2,1)}), bf16[16,24,256]{2,1,0:T(8,128)(2,1)S(1)}, u32[]{:S(2)}, u32[]{:S(2)}) async-start(bf16[16,24,256]{2,1,0:T(8,128)(2,1)} %broadcast_in_dim.18), calls=%async_computation | async-start | bytes 393216 | tf_op jit(solution)/shard_map/all_to_all | solution.py:24
  39.9 8.7 %copy-start.1 = (f32[256]{0:T(256)S(1)}, f32[256]{0:T(256)}, u32[]{:S(2)}) copy-start(f32[256]{0:T(256)} %param.6) | copy-start | bytes 3076
  40.9 19.0 %all-to-all-start.2 = ((bf16[4,416,256]{2,1,0:T(8,128)(2,1)}), bf16[4,416,256]{2,1,0:T(8,128)(2,1)S(1)}, u32[]{:S(2)}, u32[]{:S(2)}) async-start(bf16[4,416,256]{2,1,0:T(8,128)(2,1)} %pad_maximum_fusion), calls=%async_computation.2 | async-start | bytes 1703936 | tf_op jit(solution)/shard_map/all_to_all | solution.py:24
  65.7 10.5 %all-to-all-start.3 = ((f32[8,4,512]{2,1,0:T(4,128)}), f32[8,4,512]{2,1,0:T(4,128)S(1)}, u32[]{:S(2)}, u32[]{:S(2)}) async-start(f32[8,4,512]{2,1,0:T(4,128)} %reshape.93), calls=%async_computation.3 | async-start | bytes 131072 | tf_op jit(solution)/shard_map/all_to_all | solution.py:24
  69.1 2.7 %copy-start = (f32[512,512]{1,0:T(8,128)S(1)}, f32[512,512]{1,0:T(8,128)}, u32[]{:S(2)}) copy-start(f32[512,512]{1,0:T(8,128)} %get-tuple-element.23) | copy-start | bytes 3145732
  77.7 10.5 %all-to-all-start.4 = ((f32[8,4,512]{2,1,0:T(4,128)}), f32[8,4,512]{2,1,0:T(4,128)S(1)}, u32[]{:S(2)}, u32[]{:S(2)}) async-start(f32[8,4,512]{2,1,0:T(4,128)} %broadcast_in_dim.21), calls=%async_computation.4 | async-start | bytes 131072 | tf_op jit(solution)/shard_map/all_to_all | solution.py:24
  89.9 12.4 %all-to-all-start.5 = ((bf16[16,2,1024]{2,1,0:T(2,128)(2,1)}), bf16[16,2,1024]{2,1,0:T(2,128)(2,1)S(1)}, u32[]{:S(2)}, u32[]{:S(2)}) async-start(bf16[16,2,1024]{2,1,0:T(2,128)(2,1)} %reshape.96), calls=%async_computation.5 | async-start | bytes 131072 | tf_op jit(solution)/shard_map/all_to_all | solution.py:24
  115.8 10.7 %all-to-all-start.7 = ((f32[8,4,640]{2,1,0:T(4,128)}), f32[8,4,640]{2,1,0:T(4,128)S(1)}, u32[]{:S(2)}, u32[]{:S(2)}) async-start(f32[8,4,640]{2,1,0:T(4,128)} %reshape.99), calls=%async_computation.7 | async-start | bytes 163840 | tf_op jit(solution)/shard_map/all_to_all | solution.py:24

commit v3 on v2

--- a/solution.py
+++ b/solution.py
@@ -28,6 +28,10 @@
     return exchange(jnp.broadcast_to(part[None], (count,) + part.shape), axes)
 
 
+def swap(part, axis):
+    return lax.ppermute(part, axis, [(0, 1), (1, 0)])
+
+
 def scatter_sum(parts, axes):
     return jnp.sum(exchange(parts, axes).astype(f32), axis=0)
 
@@ -48,20 +52,36 @@
     group = width // n_cols
 
     part_feats = points.shape[1]
+    zl, core = lax.axis_index("zl"), lax.axis_index("core")
+    own_centres = centres.T
+    peer_centres = swap(own_centres, "zl")
+    pair = jnp.where(
+        zl == 0, jnp.stack([own_centres, peer_centres]), jnp.stack([peer_centres, own_centres])
+    )
     both = gather(jnp.concatenate([points.T, targets.T], axis=0), CTR, n_ctr)
-    some_centres = gather(centres.T, "y", n_y).reshape(-1, rows)
-    half = some_centres.shape[0]
     own_points = both[:, :part_feats].reshape(feats, rows)
-    own_targets = both[:, part_feats:].reshape(n_cols, group, rows)
-    fixed = jnp.concatenate([own_points, some_centres], axis=0)
+    own_targets = both[:, part_feats:].reshape(2, 2 * group, rows)
+    kept, given = jnp.where(zl == 0, own_targets, own_targets[::-1])
+    near = jnp.concatenate([own_points, kept], axis=0)
+    far = swap(jnp.concatenate([own_points, given], axis=0), "zl")
+    near = jnp.stack([near, far])
+    near_points = near[:, :feats]
+    near_targets = near[:, feats:].reshape(2, 2, group, rows)
+    near_targets = jnp.where(core == 0, near_targets, near_targets[:, ::-1])
+    half = gather(pair, "y", n_y).reshape(-1, rows)
     sent = jnp.concatenate(
-        [jnp.broadcast_to(fixed[None], (n_cols,) + fixed.shape), own_targets], axis=1
+        [near_points.reshape(-1, rows), near_targets[:, 1].reshape(-1, rows), half], axis=0
     )
-    got = exchange(sent, COLS)
-    points_t = got[:, :feats]
-    centres_t = got[:, feats : feats + half].reshape(2, 2, n_y, -1, cols)
-    centres_t = jnp.swapaxes(centres_t, 1, 2).reshape(feats, cols)
-    targets_t = got[:, feats + half :]
+    got = swap(sent, "core")
+    n_points, n_targets = 2 * feats, 2 * group
+    points_t = jnp.concatenate([near_points, got[:n_points].reshape(2, feats, rows)], axis=0)
+    targets_t = jnp.concatenate(
+        [near_targets[:, 0], got[n_points : n_points + n_targets].reshape(2, group, rows)], axis=0
+    )
+    half = half.reshape(n_y, 2, -1, cols)
+    other = got[n_points + n_targets :].reshape(half.shape)
+    centres_t = jnp.where(core == 0, jnp.stack([half, other], 2), jnp.stack([other, half], 2))
+    centres_t = jnp.swapaxes(centres_t, 0, 1).reshape(feats, cols)
 
     weight = precisions[:, None]
     centre_float = centres_t.astype(f32)
@@ -81,6 +101,9 @@
     kernel_tile = kernel_tile.reshape(n_cols * rows, cols)
     right = scatter_sum(right_part.reshape(n_y, group // n_y, cols), "y") / math.sqrt(total)
 
+    scaled_centres, centres_t, _ = lax.optimization_barrier(
+        (scaled_centres, centres_t, right_part)
+    )
     forward = dot(scaled_centres, centres_t, ((0,), (0,)), None)
     swapped = dot(centres_t, scaled_centres, ((0,), (0,)), None)
     squares = centre_square[:, None] + centre_square[None, :]
@@ -124,9 +147,14 @@
     step_size = norm_now[:, None] / (back[:, -128:-127] + curve_ridge[:, None])
     image = dot(back[:, :-128] + damped, root, ((1,), (0,)))
     own = jnp.concatenate([step_size * spread, gradient - step_size * image], axis=0)
-    every = gather(own, COLS + ("y",), n_pts).reshape(n_pts, 2, -1, cols)
-    every = jnp.transpose(every, (1, 3, 0, 2)).reshape(2, cols, width)
-    return every[0], every[1]
+    every = gather(own.astype(bf16), COLS + ("y",), n_pts).reshape(2 * width, cols)
+    share = width // n_pts
+    source = lax.broadcasted_iota(jnp.int32, (2 * width, 2 * width), 0)
+    target = lax.broadcasted_iota(jnp.int32, (2 * width, 2 * width), 1)
+    place = (source // share % 2) * width + source // (2 * share) * share + source % share
+    select = (place == target).astype(bf16)
+    every = dot(every, select, ((0,), (0,)), None)
+    return every[:, :width], every[:, width:]
 
 
 def solution(mesh):

time: 156 us -> 144 us (0.923)
  blocking collectives: 37.2 us -> 11.6 us
  starting transfers between devices: 41.5 us -> 62.8 us
  waiting for transfers between devices: 52 us -> 43.5 us
    all_to_all x2 -> x1, blocking collectives: 37.2 us -> 11.6 us  [exchange(): return lax.all_to_all(parts, axes, 0, 0)]
    ppermute x0 -> x3, starting transfers between devices: none -> 13.7 us  [swap(): return lax.ppermute(part, axis, [(0, 1), (1, 0)])]
    all_to_all x7, waiting for transfers between devices: 52 us -> 40.4 us  [exchange(): return lax.all_to_all(parts, axes, 0, 0)]
    all_to_all x7, starting transfers between devices: 41.5 us -> 49.2 us  [exchange(): return lax.all_to_all(parts, axes, 0, 0)]
    ppermute x0 -> x3, waiting for transfers between devices: none -> 3.18 us  [swap(): return lax.ppermute(part, axis, [(0, 1), (1, 0)])]
    dot_general x10 -> x11, matrix products: 10.9 us -> 11.4 us  [dot(): lax.dot_general(left, right, (dims, ((), ())), precision=precision, prefe...]
  transfers between devices with their start and end apart: 7 -> 10, of which waited for: 7 -> 8; matrix products, arithmetic and copies ran while one was open for 4% -> 7% of each run, Pallas kernels for 0% -> 0%
where the time goes in v3:
time: 144 us; the launch traced here: 143 us
  starting transfers between devices  62.8 us (44%)
  waiting for transfers between devices  43.5 us (30%)
  matrix products  12.6 us (9%)
  blocking collectives  11.6 us (8%)
  local copies, waits for them, and re-layouts  6.87 us (5%)
  other arithmetic  3.49 us (2%)
  between operations  1.72 us (1%)
    all_to_all x7, starting transfers between devices, exchange(): return lax.all_to_all(parts, axes, 0, 0)  49.2 us
    all_to_all x7, waiting for transfers between devices, exchange(): return lax.all_to_all(parts, axes, 0, 0)  40.4 us
    ppermute x3, starting transfers between devices, swap(): return lax.ppermute(part, axis, [(0, 1), (1, 0)])  13.7 us
    all_to_all x1, blocking collectives, exchange(): return lax.all_to_all(parts, axes, 0, 0)  11.6 us
    dot_general x11, matrix products, dot(): lax.dot_general(left, right, (dims, ((), ())), precision=precision, prefe...  11.4 us
    ppermute x3, waiting for transfers between devices, swap(): return lax.ppermute(part, axis, [(0, 1), (1, 0)])  3.18 us
  transfers between devices with their start and end apart: 10, of which 8 were waited for; matrix products, arithmetic and copies ran while one was open for 7% of the time, Pallas kernels for 0%

profile of v3, /device:TPU:1, one launch (start us, length us, event | category | flops | bytes accessed | tf_op | source)
XLA Modules:
  0.0 142.6 jit_solution(4452624166058149521)
XLA Ops:
  0.6 0.7 pad_maximum_fusion.7
  1.3 0.7 broadcast_in_dim.16
  2.0 13.4 %all-to-all-start = ((bf16[16,24,256]{2,1,0:T(8,128)(2,1)}), bf16[16,24,256]{2,1,0:T(8,128)(2,1)S(1)}, u32[]{:S(2)}, u32[]{:S(2)}) async-start(bf16[16,24,256]{2,1,0:T(8,128)(2,1)} %broadcast_in_dim.16), calls=%async_computation | async-start | bytes 393216 | tf_op jit(solution)/shard_map/all_to_all | solution.py:24
  15.5 3.1 %collective-permute-start.1 = (bf16[8,512]{1,0:T(8,128)(2,1)}, bf16[8,512]{1,0:T(8,128)(2,1)S(1)}, u32[]{:S(2)}, u32[]{:S(2)}) collective-permute-start(bf16[8,512]{1,0:T(8,128)(2,1)} %bitcast.77), channel_id=1, source_target_pairs={{0,256},{256,0},{1,257},{257,1},{2,258},{258,2},{3,259},{259,3},{4... | collective-permute-start | bytes 24584 | tf_op jit(solution)/shard_map/ppermute | solution.py:32
  18.6 1.9 %collective-permute-done.1 = bf16[8,512]{1,0:T(8,128)(2,1)S(1)} collective-permute-done((bf16[8,512]{1,0:T(8,128)(2,1)}, bf16[8,512]{1,0:T(8,128)(2,1)S(1)}, u32[]{:S(2)}, u32[]{:S(2)}) %collective-permute-start.1) | collective-permute-done | bytes 8224 | tf_op jit(solution)/shard_map/ppermute | solution.py:32
  20.5 0.8 maximum_select_fusion.1
  21.3 3.9 %all-to-all-done = bf16[16,24,256]{2,1,0:T(8,128)(2,1)S(1)} async-done(((bf16[16,24,256]{2,1,0:T(8,128)(2,1)}), bf16[16,24,256]{2,1,0:T(8,128)(2,1)S(1)}, u32[]{:S(2)}, u32[]{:S(2)}) %all-to-all-start) | async-done | bytes 196640 | tf_op jit(solution)/shard_map/all_to_all | solution.py:24
  25.8 6.8 %all-to-all-start.1 = ((bf16[8,2,8,512]{3,2,1,0:T(8,128)(2,1)}), bf16[8,2,8,512]{3,2,1,0:T(8,128)(2,1)S(1)}, u32[]{:S(2)}, u32[]{:S(2)}) async-start(bf16[8,2,8,512]{3,2,1,0:T(8,128)(2,1)} %broadcast_in_dim.17), calls=%async_computation.1 | async-start | bytes 262144 | tf_op jit(solution)/shard_map/all_to_all | solution.py:24
  32.7 3.9 %collective-permute-start = (bf16[320,256]{1,0:T(8,128)(2,1)S(1)}, bf16[320,256]{1,0:T(8,128)(2,1)S(1)}, u32[]{:S(2)}, u32[]{:S(2)}) collective-permute-start(bf16[320,256]{1,0:T(8,128)(2,1)S(1)} %get-tuple-element.13), channel_id=1, source_target_pairs={{0,256},{256,0},{1,257},{257,1},{2,258},{258,2},{3,259},{259,3},{4... | collective-permute-start | bytes 491528 | tf_op jit(solution)/shard_map/ppermute | solution.py:32
  36.7 3.9 %all-to-all-done.1 = bf16[8,2,8,512]{3,2,1,0:T(8,128)(2,1)S(1)} async-done(((bf16[8,2,8,512]{3,2,1,0:T(8,128)(2,1)}), bf16[8,2,8,512]{3,2,1,0:T(8,128)(2,1)S(1)}, u32[]{:S(2)}, u32[]{:S(2)}) %all-to-all-start.1) | async-done | bytes 131104 | tf_op jit(solution)/shard_map/all_to_all | solution.py:24
  40.8 6.6 %collective-permute-start.2 = (bf16[832,256]{1,0:T(8,128)(2,1)S(1)}, bf16[832,256]{1,0:T(8,128)(2,1)S(1)}, u32[]{:S(2)}, u32[]{:S(2)}) collective-permute-start(bf16[832,256]{1,0:T(8,128)(2,1)S(1)} %pad_maximum_fusion.1), channel_id=1, source_target_pairs={{0,16},{16,0},{1,17},{17,1},{2,18},{18,2},{3,19},{19,3},{4,20},{20... | collective-permute-start | bytes 1277960 | tf_op jit(solution)/shard_map/ppermute | solution.py:32
  47.5 1.2 collective-permute-done.2
  49.3 0.8 multiply_convert_fusion.2
  50.1 0.7 negate_exponential_fusion
  52.0 5.1 %all-to-all-start.2 = ((f32[8,4,512]{2,1,0:T(4,128)}), f32[8,4,512]{2,1,0:T(4,128)S(1)}, u32[]{:S(2)}, u32[]{:S(2)}) async-start(f32[8,4,512]{2,1,0:T(4,128)} %reshape.135), calls=%async_computation.2 | async-start | bytes 131072 | tf_op jit(solution)/shard_map/all_to_all | solution.py:24
  57.5 2.3 %multiply_reduce_fusion = (f32[]{:T(128)}, f32[512,512]{1,0:T(8,128)S(1)}) fusion(f32[512,512]{1,0:T(8,128)S(1)} %fusion.6, bf16[256,512]{1,0:T(8,128)(2,1)} %multiply_convert_fusion.2, bf16[256,512]{1,0:T(8,128)(2,1)S(1)} %bitcast.66, f32[512]{0:T(512)S(1)} %get-tuple-element.8), kind=kOutput, calls=%fused_computation.25 | convolution fusion | flops 137101312 | bytes 2623492 | tf_op jit(solution)/shard_map/dot_general | solution.py:18
  60.7 1.0 fusion.17
  61.8 2.8 %convolution_add_fusion = f32[512,512]{1,0:T(8,128)S(1)} fusion(f32[512,512]{1,0:T(8,128)S(1)} %fusion.17, f32[512,512]{1,0:T(8,128)} %copy-done, f32[]{:T(128)S(6)} %sqrt.3), kind=kOutput, calls=%fused_computation.5 | convolution fusion | flops 808452096 | bytes 3145732 | tf_op jit(solution)/shard_map/dot_general | solution.py:18
  66.0 6.6 %all-to-all-start.3 = ((f32[8,4,512]{2,1,0:T(4,128)}), f32[8,4,512]{2,1,0:T(4,128)S(1)}, u32[]{:S(2)}, u32[]{:S(2)}) async-start(f32[8,4,512]{2,1,0:T(4,128)} %broadcast_in_dim.18), calls=%async_computation.3 | async-start | bytes 131072 | tf_op jit(solution)/shard_map/all_to_all | solution.py:24
  72.7 1.7 %multiply_reduce_fusion.2 = (f32[4]{0:T(128)S(1)}, f32[4,512]{1,0:T(4,128)S(1)}) fusion(f32[4,512]{1,0:T(4,128)S(1)} %fusion.69, f32[512,512]{1,0:T(8,128)} %copy-done), kind=kOutput, calls=%fused_computation.88 | convolution fusion | flops 6297596 | bytes 1064976 | tf_op jit(solution)/shard_map/dot_general | solution.py:18
  74.5 5.5 %all-to-all-done.3 = f32[8,4,512]{2,1,0:T(4,128)S(1)} async-done(((f32[8,4,512]{2,1,0:T(4,128)}), f32[8,4,512]{2,1,0:T(4,128)S(1)}, u32[]{:S(2)}, u32[]{:S(2)}) %all-to-all-start.3) | async-done | bytes 65568 | tf_op jit(solution)/shard_map/all_to_all | solution.py:24
  79.9 1.0 convolution_convert_fusion
  81.0 0.7 reshape.138
  81.6 3.8 %all-to-all-start.4 = ((bf16[16,2,1024]{2,1,0:T(2,128)(2,1)}), bf16[16,2,1024]{2,1,0:T(2,128)(2,1)S(1)}, u32[]{:S(2)}, u32[]{:S(2)}) async-start(bf16[16,2,1024]{2,1,0:T(2,128)(2,1)} %reshape.138), calls=%async_computation.4 | async-start | bytes 131072 | tf_op jit(solution)/shard_map/all_to_all | solution.py:24
  85.6 8.9 %all-to-all-done.4 = bf16[16,2,1024]{2,1,0:T(2,128)(2,1)S(1)} async-done(((bf16[16,2,1024]{2,1,0:T(2,128)(2,1)}), bf16[16,2,1024]{2,1,0:T(2,128)(2,1)S(1)}, u32[]{:S(2)}, u32[]{:S(2)}) %all-to-all-start.4) | async-done | bytes 65568 | tf_op jit(solution)/shard_map/all_to_all | solution.py:24
  94.6 11.6 %all_to_all.40 = bf16[16,2,1152]{2,1,0:T(2,128)(2,1)S(1)} all-to-all(bf16[16,2,1152]{2,1,0:T(2,128)(2,1)S(1)} %broadcast_in_dim.20), channel_id=1, replica_groups=mesh['zl'=2,'y'=8,'core'=2,'zh'=4,'x'=4] {'zh','x'}, dimensions={0} | all-to-all | bytes 147456 | tf_op jit(solution)/shard_map/all_to_all | solution.py:24
  107.9 3.4 %all-to-all-start.6 = ((f32[8,4,640]{2,1,0:T(4,128)}), f32[8,4,640]{2,1,0:T(4,128)S(1)}, u32[]{:S(2)}, u32[]{:S(2)}) async-start(f32[8,4,640]{2,1,0:T(4,128)} %reshape.141), calls=%async_computation.6 | async-start | bytes 163840 | tf_op jit(solution)/shard_map/all_to_all | solution.py:24
  111.5 7.1 %all-to-all-done.6 = f32[8,4,640]{2,1,0:T(4,128)S(1)} async-done(((f32[8,4,640]{2,1,0:T(4,128)}), f32[8,4,640]{2,1,0:T(4,128)S(1)}, u32[]{:S(2)}, u32[]{:S(2)}) %all-to-all-start.6) | async-done | bytes 81952 | tf_op jit(solution)/shard_map/all_to_all | solution.py:24
  119.2 0.7 broadcast_in_dim.23
  120.0 10.0 %all-to-all-start.7 = ((bf16[32,8,512]{2,1,0:T(8,128)(2,1)}), bf16[32,8,512]{2,1,0:T(8,128)(2,1)S(1)}, u32[]{:S(2)}, u32[]{:S(2)}) async-start(bf16[32,8,512]{2,1,0:T(8,128)(2,1)} %broadcast_in_dim.23), calls=%async_computation.7 | async-start | bytes 524288 | tf_op jit(solution)/shard_map/all_to_all | solution.py:24
  130.0 11.1 %all-to-all-done.7 = bf16[32,8,512]{2,1,0:T(8,128)(2,1)S(1)} async-done(((bf16[32,8,512]{2,1,0:T(8,128)(2,1)}), bf16[32,8,512]{2,1,0:T(8,128)(2,1)S(1)}, u32[]{:S(2)}, u32[]{:S(2)}) %all-to-all-start.7) | async-done | bytes 262176 | tf_op jit(solution)/shard_map/all_to_all | solution.py:24
  141.8 0.8 fusion.68
  (76 shorter events, 8.3 us)
Async XLA Ops:
  2.0 23.1 %all-to-all-start = ((bf16[16,24,256]{2,1,0:T(8,128)(2,1)}), bf16[16,24,256]{2,1,0:T(8,128)(2,1)S(1)}, u32[]{:S(2)}, u32[]{:S(2)}) async-start(bf16[16,24,256]{2,1,0:T(8,128)(2,1)} %broadcast_in_dim.16), calls=%async_computation | async-start | bytes 393216 | tf_op jit(solution)/shard_map/all_to_all | solution.py:24
  15.5 32.0 %copy-start.3 = (f32[256]{0:T(256)S(1)}, f32[256]{0:T(256)}, u32[]{:S(2)}) copy-start(f32[256]{0:T(256)} %param.6) | copy-start | bytes 3076
  15.5 5.0 %collective-permute-start.1 = (bf16[8,512]{1,0:T(8,128)(2,1)}, bf16[8,512]{1,0:T(8,128)(2,1)S(1)}, u32[]{:S(2)}, u32[]{:S(2)}) collective-permute-start(bf16[8,512]{1,0:T(8,128)(2,1)} %bitcast.77), channel_id=1, source_target_pairs={{0,256},{256,0},{1,257},{257,1},{2,258},{258,2},{3,259},{259,3},{4... | collective-permute-start | bytes 24584 | tf_op jit(solution)/shard_map/ppermute | solution.py:32
  25.8 14.8 %all-to-all-start.1 = ((bf16[8,2,8,512]{3,2,1,0:T(8,128)(2,1)}), bf16[8,2,8,512]{3,2,1,0:T(8,128)(2,1)S(1)}, u32[]{:S(2)}, u32[]{:S(2)}) async-start(bf16[8,2,8,512]{3,2,1,0:T(8,128)(2,1)} %broadcast_in_dim.17), calls=%async_computation.1 | async-start | bytes 262144 | tf_op jit(solution)/shard_map/all_to_all | solution.py:24
  32.7 7.9 %collective-permute-start = (bf16[320,256]{1,0:T(8,128)(2,1)S(1)}, bf16[320,256]{1,0:T(8,128)(2,1)S(1)}, u32[]{:S(2)}, u32[]{:S(2)}) collective-permute-start(bf16[320,256]{1,0:T(8,128)(2,1)S(1)} %get-tuple-element.13), channel_id=1, source_target_pairs={{0,256},{256,0},{1,257},{257,1},{2,258},{258,2},{3,259},{259,3},{4... | collective-permute-start | bytes 491528 | tf_op jit(solution)/shard_map/ppermute | solution.py:32
  40.8 8.0 %collective-permute-start.2 = (bf16[832,256]{1,0:T(8,128)(2,1)S(1)}, bf16[832,256]{1,0:T(8,128)(2,1)S(1)}, u32[]{:S(2)}, u32[]{:S(2)}) collective-permute-start(bf16[832,256]{1,0:T(8,128)(2,1)S(1)} %pad_maximum_fusion.1), channel_id=1, source_target_pairs={{0,16},{16,0},{1,17},{17,1},{2,18},{18,2},{3,19},{19,3},{4,20},{20... | collective-permute-start | bytes 1277960 | tf_op jit(solution)/shard_map/ppermute | solution.py:32
  48.8 1.3 copy-start.1
  50.1 0.8 slice-start
  50.8 6.3 %copy-start.2 = (bf16[256,512]{1,0:T(8,128)(2,1)S(1)}, bf16[256,512]{1,0:T(8,128)(2,1)}, u32[]{:S(2)}) copy-start(bf16[256,512]{1,0:T(8,128)(2,1)} %multiply_convert_fusion.2) | copy-start | bytes 786436
  52.0 12.5 %all-to-all-start.2 = ((f32[8,4,512]{2,1,0:T(4,128)}), f32[8,4,512]{2,1,0:T(4,128)S(1)}, u32[]{:S(2)}, u32[]{:S(2)}) async-start(f32[8,4,512]{2,1,0:T(4,128)} %reshape.135), calls=%async_computation.2 | async-start | bytes 131072 | tf_op jit(solution)/shard_map/all_to_all | solution.py:24
  59.8 1.0 copy-start
  66.0 13.9 %all-to-all-start.3 = ((f32[8,4,512]{2,1,0:T(4,128)}), f32[8,4,512]{2,1,0:T(4,128)S(1)}, u32[]{:S(2)}, u32[]{:S(2)}) async-start(f32[8,4,512]{2,1,0:T(4,128)} %broadcast_in_dim.18), calls=%async_computation.3 | async-start | bytes 131072 | tf_op jit(solution)/shard_map/all_to_all | solution.py:24
  81.6 12.8 %all-to-all-start.4 = ((bf16[16,2,1024]{2,1,0:T(2,128)(2,1)}), bf16[16,2,1024]{2,1,0:T(2,128)(2,1)S(1)}, u32[]{:S(2)}, u32[]{:S(2)}) async-start(bf16[16,2,1024]{2,1,0:T(2,128)(2,1)} %reshape.138), calls=%async_computation.4 | async-start | bytes 131072 | tf_op jit(solution)/shard_map/all_to_all | solution.py:24
  107.9 10.7 %all-to-all-start.6 = ((f32[8,4,640]{2,1,0:T(4,128)}), f32[8,4,640]{2,1,0:T(4,128)S(1)}, u32[]{:S(2)}, u32[]{:S(2)}) async-start(f32[8,4,640]{2,1,0:T(4,128)} %reshape.141), calls=%async_computation.6 | async-start | bytes 163840 | tf_op jit(solution)/shard_map/all_to_all | solution.py:24
  120.0 21.2 %all-to-all-start.7 = ((bf16[32,8,512]{2,1,0:T(8,128)(2,1)}), bf16[32,8,512]{2,1,0:T(8,128)(2,1)S(1)}, u32[]{:S(2)}, u32[]{:S(2)}) async-start(bf16[32,8,512]{2,1,0:T(8,128)(2,1)} %broadcast_in_dim.23), calls=%async_computation.7 | async-start | bytes 524288 | tf_op jit(solution)/shard_map/all_to_all | solution.py:24
